TPU v7x, 256 devices: a whole 4x4x8 slice. The times are simulated.
256 devices in a mesh: row: 32 (over z, x), src: 8 (over y, core).
Axes of the slice: x: 4, y: 4, z: 8, core: 2. Of those that a mesh axis runs over, the one named last changes fastest.
Arguments:
- sub_source: float32 [32768, 4096], P('row', 'src'), may hold values from -6 to 6
- sub_inverse: bfloat16 [32768, 1024], P('row'), as said below
- coupling: bfloat16 [32, 2, 512, 1024], P('row'), may hold values from -0.0625 to 0.0625
- update_lists: int32 [32, 2], P('row'), may hold values from 0 to 3, as said below
- sep_source: float32 [2048, 4096], P('row', 'src'), may hold values from -6 to 6
- sep_inverse: bfloat16 [16384, 512], P(('row', 'src')), as said below
- sep_lower: bfloat16 [16384, 1024], P(('row', 'src')), may hold values from -0.125 to 0.125
- factor_owner_slots: int32 [4], replicated, may hold values from 0 to 31, as said below
- sep_links: int32 [4, 2], replicated, may hold values from -1 to 2, as said below
Outputs:
- sub_field: float32 [32768, 4096], P('row', 'src')
- sep_field: float32 [2048, 4096], P('row', 'src')
Inputs may be any that keep to these rules, and one draw needn't show every extreme that they name: `update_lists`: each subtree lists two different separator blocks. `factor_owner_slots`: the 4 entries are different slots. `sep_links`: for block k the first entry is k - 1 and the second is -1 or a block below k - 1; -1 means no link. `sub_inverse`: each slot of 1024 rows is lower triangular. `sep_inverse`: each slot of 512 rows is lower triangular.
All inputs are finite; a program needn't handle non-finite values.
Results may differ from a plain program's by a relative error of at most 0.006.
Values may be sent and summed in bfloat16 or wider, within the bound.
A program may use at most 64 MiB of HBM per device.

v0:
```python
import jax
import jax.numpy as jnp
from jax import lax
from jax.sharding import PartitionSpec as P

SEP_BLOCK = 512
STEPS = 4
LINKS = 2
SEP_ROWS = 2048


def from_root(shard, axis, root):
    mine = lax.axis_index(axis) == root
    return lax.psum(jnp.where(mine, shard, jnp.zeros_like(shard)), axis)


def per_device(
    sub_source,
    sub_inverse,
    coupling,
    update_lists,
    sep_source,
    sep_inverse,
    sep_lower,
    factor_owner_slots,
    sep_links,
):
    sources = sub_source.shape[1]
    sub_field = jnp.dot(
        sub_inverse, sub_source.astype(jnp.bfloat16), preferred_element_type=jnp.float32
    )
    padded_length = sub_field.astype(jnp.bfloat16)
    pending_updates = jnp.einsum(
        "rmf,ft->rmt", coupling[0], padded_length, preferred_element_type=jnp.float32
    )
    picks = update_lists[0][:, None] == jnp.arange(STEPS, dtype=jnp.int32)[None, :]
    dense = jnp.sum(jnp.where(picks[:, :, None, None], pending_updates[:, None], 0.0), axis=0)
    local_rows = sep_source.shape[0]
    my_row = lax.axis_index("row")
    placed = lax.dynamic_update_slice(
        jnp.zeros((SEP_ROWS, sources), jnp.float32),
        sep_source,
        (my_row * local_rows, jnp.zeros((), jnp.int32)),
    )
    terms = placed - dense.reshape(SEP_ROWS, sources)
    totals = lax.psum(terms, "row")
    inverse_row_block, lower_rows = (
        lax.all_gather(sep_inverse, "src", axis=0, tiled=True),
        lax.all_gather(sep_lower, "src", axis=0, tiled=True),
    )
    solved = jnp.zeros((STEPS, SEP_BLOCK, sources), jnp.float32)
    for block_id in range(STEPS):
        pending = totals[block_id * SEP_BLOCK : (block_id + 1) * SEP_BLOCK]
        pieces = []
        for link_pos in range(LINKS):
            target = sep_links[block_id, link_pos]
            chosen = solved[jnp.maximum(target, 0)]
            pieces.append(jnp.where(target >= 0, chosen, 0.0).astype(jnp.bfloat16))
        stacked = jnp.concatenate(pieces, axis=0)
        remaining_source = pending - jnp.dot(
            lower_rows, stacked, preferred_element_type=jnp.float32
        )
        candidate = jnp.dot(
            inverse_row_block,
            remaining_source.astype(jnp.bfloat16),
            preferred_element_type=jnp.float32,
        )
        result = from_root(candidate, "row", factor_owner_slots[block_id])
        solved = solved.at[block_id].set(result)
    whole_field = solved.reshape(SEP_ROWS, sources)
    own_rows = lax.dynamic_slice_in_dim(whole_field, my_row * local_rows, local_rows, 0)
    return (sub_field, own_rows)


def solution(mesh):
    return jax.shard_map(
        per_device,
        mesh=mesh,
        in_specs=(
            P("row", "src"),
            P("row", None),
            P("row", None, None, None),
            P("row", None),
            P("row", "src"),
            P(("row", "src"), None),
            P(("row", "src"), None),
            P(),
            P(),
        ),
        out_specs=(P("row", "src"), P("row", "src")),
        check_vma=False,
    )
```

profile of v0, /device:TPU:8, one launch (start us, length us, event | category | flops | bytes accessed | tf_op | source)
XLA Modules:
  0.0 840.7 jit_solution(14617722687658571348)
XLA Ops:
  8.1 0.7 all-gather.2.cloned.1.call-update
  8.8 1.0 copy.16
  9.9 3.0 fusion.32
  12.9 1.3 copy-done.8
  14.2 2.6 fusion.2
  16.8 2.9 copy.18
  19.8 4.9 select_reduce_fusion
  24.7 5.4 copy.23
  30.1 2.5 broadcast_in_dim.36
  32.6 1.8 dynamic_update_slice.3
  34.4 6.7 sub.15
  41.7 0.7 fusion.55
  43.1 13.3 %all_gather.7 = bf16[512,512]{1,0:T(8,128)(2,1)S(1)} all-gather(bf16[64,512]{1,0:T(8,128)(2,1)S(1)} %copy-done.3), channel_id=1, replica_groups=mesh['row'=32,'src'=8] {'src'}, dimensions={0}, use_global_device_ids=true | all-gather | bytes 589824 | tf_op jit(solution)/shard_map/all_gather | solution.py:48
  56.4 152.0 %all-reduce.8.cloned.1.call-done = f32[2048,512]{0,1:T(8,128)} async-done(((f32[2048,512]{0,1:T(8,128)}), f32[2048,512]{0,1:T(8,128)}) %all-reduce.8.cloned.1.call-update) | async-done | bytes 4194320 | tf_op jit(solution)/shard_map/psum | solution.py:46
  208.4 3.8 fusion.8
  212.3 0.7 fusion.54
  215.9 143.8 %all-reduce.10.cloned.1.call-done = f32[1,512,512]{1,2,0:T(8,128)} async-done(((f32[1,512,512]{1,2,0:T(8,128)}), f32[1,512,512]{1,2,0:T(8,128)}) %all-reduce.10.cloned.1.call-update) | async-done | bytes 1048592 | tf_op jit(solution)/shard_map/psum | solution.py:14
  359.7 2.7 fusion.45
  362.5 4.0 fusion.7
  369.7 2.6 scatter.14
  372.3 141.5 %all-reduce.12.cloned.1.call-done = f32[1,512,512]{1,2,0:T(8,128)} async-done(((f32[1,512,512]{1,2,0:T(8,128)}), f32[1,512,512]{1,2,0:T(8,128)}) %all-reduce.12.cloned.1.call-update) | async-done | bytes 1048592 | tf_op jit(solution)/shard_map/psum | solution.py:14
  513.8 2.3 constant_dynamic-update-slice_fusion.2
  516.1 1.8 fusion.40
  517.9 3.7 fusion.6
  524.7 144.2 %all-reduce.14.cloned.1.call-done = f32[1,512,512]{1,2,0:T(8,128)} async-done(((f32[1,512,512]{1,2,0:T(8,128)}), f32[1,512,512]{1,2,0:T(8,128)}) %all-reduce.14.cloned.1.call-update) | async-done | bytes 1048592 | tf_op jit(solution)/shard_map/psum | solution.py:14
  668.9 2.3 constant_dynamic-update-slice_fusion.1
  671.2 1.8 fusion.42
  673.0 3.7 fusion.5
  676.7 147.3 %all-reduce.16.cloned.1.call-done = f32[1,512,512]{1,2,0:T(8,128)} async-done(((f32[1,512,512]{1,2,0:T(8,128)}), f32[1,512,512]{1,2,0:T(8,128)}) %all-reduce.16.cloned.1.call-update) | async-done | bytes 1048592 | tf_op jit(solution)/shard_map/psum | solution.py:14
  824.1 2.3 constant_dynamic-update-slice_fusion
  826.3 5.2 copy.20
  831.6 1.6 constant_dynamic-slice_fusion
  (32 shorter events, 1.0 us)
Async XLA Ops:
  8.0 1.8 copy-start
  8.0 48.4 %all-gather.2.cloned.1.call-start = ((), (), s32[]{:S(2)}) async-start(), calls=%async_computation.1 | async-start | bytes 1179648 | tf_op jit(solution)/shard_map/all_gather | solution.py:49
  8.7 199.7 %all-reduce.8.cloned.1.call-start = ((), (), s32[]{:S(2)}) async-start(), calls=%async_computation | async-start | bytes 8388608 | tf_op jit(solution)/shard_map/psum | solution.py:46
  9.8 4.3 copy-start.6
  12.8 1.3 copy-start.8
  14.2 5.6 copy-start.7
  41.1 0.7 copy-start.5
  41.1 2.0 copy-start.3
  41.1 171.2 %copy-start.4 = (s32[4,2]{0,1:T(2,128)S(1)}, s32[4,2]{0,1:T(2,128)}, u32[]{:S(2)}) copy-start(s32[4,2]{0,1:T(2,128)} %param.25) | copy-start | bytes 100
  41.1 318.6 %all-reduce.10.cloned.1.call-start = ((), (), s32[]{:S(2)}) async-start(), calls=%async_computation.2 | async-start | bytes 2097152 | tf_op jit(solution)/shard_map/psum | solution.py:14
  56.4 303.3 %copy-start.2 = (bf16[512,512]{1,0:T(8,128)(2,1)}, bf16[512,512]{1,0:T(8,128)(2,1)S(1)}, u32[]{:S(2)}) copy-start(bf16[512,512]{1,0:T(8,128)(2,1)S(1)} %all_gather.7) | copy-start | bytes 1572868
  212.2 301.6 %all-reduce.12.cloned.1.call-start = ((), (), s32[]{:S(2)}) async-start(), calls=%async_computation.3 | async-start | bytes 2097152 | tf_op jit(solution)/shard_map/psum | solution.py:14
  359.7 10.0 %copy-start.1 = (f32[1,512,512]{1,2,0:T(8,128)S(1)}, f32[1,512,512]{1,2,0:T(8,128)}, u32[]{:S(2)}) copy-start(f32[1,512,512]{1,2,0:T(8,128)} %all-reduce.10.cloned.1.call-done) | copy-start | bytes 3145732
  366.5 302.4 %all-reduce.14.cloned.1.call-start = ((), (), s32[]{:S(2)}) async-start(), calls=%async_computation.4 | async-start | bytes 2097152 | tf_op jit(solution)/shard_map/psum | solution.py:14
  521.6 302.5 %all-reduce.16.cloned.1.call-start = ((), (), s32[]{:S(2)}) async-start(), calls=%async_computation.5 | async-start | bytes 2097152 | tf_op jit(solution)/shard_map/psum | solution.py:14
Sparse Core Ops, SparseCore 0:
  10.7 27.0 all-gather.1
Sparse Core Ops, SparseCore 1:
  41.2 167.2 all-reduce.7
  212.3 147.3 all-reduce.9
  366.6 147.2 all-reduce.11
  521.6 147.2 all-reduce.13
  676.8 147.2 all-reduce.15
where the time goes:
time: 842 us; the launch traced here: 841 us
  waiting for transfers between devices  730 us (87%)
  local copies, waits for them, and re-layouts  33.2 us (4%)
  between operations  25.6 us (3%)
  matrix products  20.7 us (2%)
  other arithmetic  18 us (2%)
  blocking collectives  13.3 us (2%)
    psum x4, waiting for transfers between devices, from_root(): return lax.psum(jnp.where(mine, shard, jnp.zeros_like(shard)), axis)  577 us
    psum x1, waiting for transfers between devices, per_device(): totals = lax.psum(terms, 'row')  152 us
  transfers between devices with their start and end apart: 6, of which 5 were waited for; matrix products, arithmetic and copies ran while one was open for 4% of the time, Pallas kernels for 0%

commit v1 on v0

--- a/solution.py
+++ b/solution.py
@@ -43,7 +43,19 @@
         (my_row * local_rows, jnp.zeros((), jnp.int32)),
     )
     terms = placed - dense.reshape(SEP_ROWS, sources)
-    totals = lax.psum(terms, "row")
+
+    def _link_quotas(state):
+        along_axis = "row"
+        how_many = lax.axis_size(along_axis)
+        everything = lambda work_now: [(jj, jj ^ work_now) for jj in range(how_many)]
+        raw_out = state
+        for tick in range(how_many.bit_length() - 1):
+            r_now = everything(1 << tick)
+            big = lax.ppermute(raw_out, axis_name=along_axis, perm=r_now)
+            raw_out = raw_out + big
+        return raw_out
+
+    totals = _link_quotas(terms)
     inverse_row_block, lower_rows = (
         lax.all_gather(sep_inverse, "src", axis=0, tiled=True),
         lax.all_gather(sep_lower, "src", axis=0, tiled=True),

time: 842 us -> 1330 us (1.58)
  waiting for transfers between devices: 730 us -> 1190 us
  starting transfers between devices: 0.26 us -> 16.7 us
    ppermute x0 -> x5, waiting for transfers between devices: none -> 615 us  [_link_quotas(): big = lax.ppermute(raw_out, axis_name=along_axis, perm=r_now)]
    psum x1 -> x0, waiting for transfers between devices: 152 us -> none  [per_device(): totals = lax.psum(terms, 'row')]
    ppermute x0 -> x5, starting transfers between devices: none -> 16.5 us  [_link_quotas(): big = lax.ppermute(raw_out, axis_name=along_axis, perm=r_now)]
  transfers between devices with their start and end apart: 6 -> 10, of which waited for: 5 -> 9; matrix products, arithmetic and copies ran while one was open for 4% -> 1% of each run, Pallas kernels for 0% -> 0%
where the time goes in v1:
time: 1330 us
  waiting for transfers between devices  1190 us (89%)
  local copies, waits for them, and re-layouts  32.4 us (2%)
  other arithmetic  25.1 us (2%)
  between operations  24 us (2%)
  matrix products  19.4 us (1%)
  starting transfers between devices  16.7 us (1%)
  blocking collectives  13.5 us (1%)
    ppermute x5, waiting for transfers between devices, _link_quotas(): big = lax.ppermute(raw_out, axis_name=along_axis, perm=r_now)  615 us
    psum x4, waiting for transfers between devices, from_root(): return lax.psum(jnp.where(mine, shard, jnp.zeros_like(shard)), axis)  579 us
  transfers between devices with their start and end apart: 10, of which 9 were waited for; matrix products, arithmetic and copies ran while one was open for 1% of the time, Pallas kernels for 0%

profile of v1, /device:TPU:8, one launch (start us, length us, event | category | flops | bytes accessed | tf_op | source)
XLA Modules:
  0.0 1325.3 jit_solution(12672322021810233946)
XLA Ops:
  8.8 3.0 fusion.34
  13.1 2.7 fusion.2
  15.8 1.9 copy.18
  17.8 2.9 select_reduce_fusion
  20.7 5.4 copy.23
  26.1 2.5 broadcast_in_dim.36
  30.4 4.2 sub.15
  36.6 90.6 %collective-permute-done = f32[2048,512]{0,1:T(8,128)S(1)} collective-permute-done((f32[2048,512]{0,1:T(8,128)S(1)}, f32[2048,512]{0,1:T(8,128)S(1)}, u32[]{:S(2)}, u32[]{:S(2)}) %collective-permute-start) | collective-permute-done | bytes 4194336 | tf_op jit(solution)/shard_map/ppermute | solution.py:54
  128.2 3.0 collective-permute-start.1
  131.3 90.1 %collective-permute-done.1 = f32[2048,512]{0,1:T(8,128)S(1)} collective-permute-done((f32[2048,512]{0,1:T(8,128)S(1)}, f32[2048,512]{0,1:T(8,128)S(1)}, u32[]{:S(2)}, u32[]{:S(2)}) %collective-permute-start.1) | collective-permute-done | bytes 4194336 | tf_op jit(solution)/shard_map/ppermute | solution.py:54
  222.5 2.0 collective-permute-start.2
  224.4 88.9 %collective-permute-done.2 = f32[2048,512]{0,1:T(8,128)S(1)} collective-permute-done((f32[2048,512]{0,1:T(8,128)S(1)}, f32[2048,512]{0,1:T(8,128)S(1)}, u32[]{:S(2)}, u32[]{:S(2)}) %collective-permute-start.2) | collective-permute-done | bytes 4194336 | tf_op jit(solution)/shard_map/ppermute | solution.py:54
  314.5 3.4 collective-permute-start.3
  317.9 178.2 %collective-permute-done.3 = f32[2048,512]{0,1:T(8,128)S(1)} collective-permute-done((f32[2048,512]{0,1:T(8,128)S(1)}, f32[2048,512]{0,1:T(8,128)S(1)}, u32[]{:S(2)}, u32[]{:S(2)}) %collective-permute-start.3) | collective-permute-done | bytes 4194336 | tf_op jit(solution)/shard_map/ppermute | solution.py:54
  496.1 2.7 add.49
  498.8 6.2 collective-permute-start.4
  506.3 13.5 %all_gather.7 = bf16[512,512]{1,0:T(8,128)(2,1)S(1)} all-gather(bf16[64,512]{1,0:T(8,128)(2,1)S(1)} %copy-done.3), channel_id=1, replica_groups=mesh['row'=32,'src'=8] {'src'}, dimensions={0}, use_global_device_ids=true | all-gather | bytes 589824 | tf_op jit(solution)/shard_map/all_gather | solution.py:60
  519.8 166.8 %collective-permute-done.4 = f32[2048,512]{0,1:T(8,128)} collective-permute-done((f32[2048,512]{0,1:T(8,128)}, f32[2048,512]{0,1:T(8,128)}, u32[]{:S(2)}, u32[]{:S(2)}) %collective-permute-start.4) | collective-permute-done | bytes 4194336 | tf_op jit(solution)/shard_map/ppermute | solution.py:54
  686.6 6.5 add.50
  693.1 3.8 fusion.8
  700.9 145.0 %all-reduce.7.cloned.1.call-done = f32[1,512,512]{1,2,0:T(8,128)} async-done(((f32[1,512,512]{1,2,0:T(8,128)}), f32[1,512,512]{1,2,0:T(8,128)}) %all-reduce.7.cloned.1.call-update) | async-done | bytes 1048592 | tf_op jit(solution)/shard_map/psum | solution.py:14
  847.7 3.5 fusion.7
  854.6 2.6 scatter.14
  857.2 141.9 %all-reduce.9.cloned.1.call-done = f32[1,512,512]{1,2,0:T(8,128)} async-done(((f32[1,512,512]{1,2,0:T(8,128)}), f32[1,512,512]{1,2,0:T(8,128)}) %all-reduce.9.cloned.1.call-update) | async-done | bytes 1048592 | tf_op jit(solution)/shard_map/psum | solution.py:14
  999.1 2.3 constant_dynamic-update-slice_fusion.2
  1003.2 3.2 fusion.6
  1009.5 144.7 %all-reduce.11.cloned.1.call-done = f32[1,512,512]{1,2,0:T(8,128)} async-done(((f32[1,512,512]{1,2,0:T(8,128)}), f32[1,512,512]{1,2,0:T(8,128)}) %all-reduce.11.cloned.1.call-update) | async-done | bytes 1048592 | tf_op jit(solution)/shard_map/psum | solution.py:14
  1154.2 2.3 constant_dynamic-update-slice_fusion.1
  1158.4 3.2 fusion.5
  1161.6 147.8 %all-reduce.13.cloned.1.call-done = f32[1,512,512]{1,2,0:T(8,128)} async-done(((f32[1,512,512]{1,2,0:T(8,128)}), f32[1,512,512]{1,2,0:T(8,128)}) %all-reduce.13.cloned.1.call-update) | async-done | bytes 1048592 | tf_op jit(solution)/shard_map/psum | solution.py:14
  1309.4 2.5 constant_dynamic-update-slice_fusion
  1311.9 5.2 copy.20
  (46 shorter events, 18.6 us)
Async XLA Ops:
  7.2 1.7 copy-start
  7.2 685.9 %all-gather.2.cloned.1.call-start = ((), (), s32[]{:S(2)}) async-start(), calls=%async_computation | async-start | bytes 1179648 | tf_op jit(solution)/shard_map/all_gather | solution.py:61
  8.8 4.3 copy-start.6
  11.8 1.3 copy-start.9
  13.1 4.6 copy-start.8
  34.7 92.5 %collective-permute-start = (f32[2048,512]{0,1:T(8,128)S(1)}, f32[2048,512]{0,1:T(8,128)S(1)}, u32[]{:S(2)}, u32[]{:S(2)}) collective-permute-start(f32[2048,512]{0,1:T(8,128)S(1)} %sub.15), channel_id=1, source_target_pairs={{0,8},{8,0},{16,24},{24,16},{32,40},{40,32},{48,56},{56,48},{64,72... | collective-permute-start | bytes 12582920 | tf_op jit(solution)/shard_map/ppermute | solution.py:54
  128.2 93.1 %collective-permute-start.1 = (f32[2048,512]{0,1:T(8,128)S(1)}, f32[2048,512]{0,1:T(8,128)S(1)}, u32[]{:S(2)}, u32[]{:S(2)}) collective-permute-start(f32[2048,512]{0,1:T(8,128)S(1)} %add.46), channel_id=1, source_target_pairs={{0,16},{8,24},{16,0},{24,8},{32,48},{40,56},{48,32},{56,40},{64,80... | collective-permute-start | bytes 12582920 | tf_op jit(solution)/shard_map/ppermute | solution.py:54
  222.5 90.9 %collective-permute-start.2 = (f32[2048,512]{0,1:T(8,128)S(1)}, f32[2048,512]{0,1:T(8,128)S(1)}, u32[]{:S(2)}, u32[]{:S(2)}) collective-permute-start(f32[2048,512]{0,1:T(8,128)S(1)} %add.47), channel_id=1, source_target_pairs={{0,32},{8,40},{16,48},{24,56},{32,0},{40,8},{48,16},{56,24},{64,96... | collective-permute-start | bytes 12582920 | tf_op jit(solution)/shard_map/ppermute | solution.py:54
  314.4 190.6 %copy-start.5 = (s32[4]{0:T(128)S(1)}, s32[4]{0:T(128)}, u32[]{:S(2)}) copy-start(s32[4]{0:T(128)} %param.24) | copy-start | bytes 52
  314.5 191.8 %copy-start.3 = (bf16[64,512]{1,0:T(8,128)(2,1)S(1)}, bf16[64,512]{1,0:T(8,128)(2,1)}, u32[]{:S(2)}) copy-start(bf16[64,512]{1,0:T(8,128)(2,1)} %param.22) | copy-start | bytes 196612
  314.5 181.6 %collective-permute-start.3 = (f32[2048,512]{0,1:T(8,128)S(1)}, f32[2048,512]{0,1:T(8,128)S(1)}, u32[]{:S(2)}, u32[]{:S(2)}) collective-permute-start(f32[2048,512]{0,1:T(8,128)S(1)} %add.48), channel_id=1, source_target_pairs={{0,64},{8,72},{16,80},{24,88},{32,96},{40,104},{48,112},{56,120},{... | collective-permute-start | bytes 12582920 | tf_op jit(solution)/shard_map/ppermute | solution.py:54
  498.8 187.8 %collective-permute-start.4 = (f32[2048,512]{0,1:T(8,128)}, f32[2048,512]{0,1:T(8,128)}, u32[]{:S(2)}, u32[]{:S(2)}) collective-permute-start(f32[2048,512]{0,1:T(8,128)} %add.49), channel_id=1, source_target_pairs={{0,128},{8,136},{16,144},{24,152},{32,160},{40,168},{48,176},{56,1... | collective-permute-start | bytes 12582920 | tf_op jit(solution)/shard_map/ppermute | solution.py:54
  505.0 340.9 %all-reduce.7.cloned.1.call-start = ((), (), s32[]{:S(2)}) async-start(), calls=%async_computation.1 | async-start | bytes 2097152 | tf_op jit(solution)/shard_map/psum | solution.py:14
  693.1 3.9 copy-start.4
  696.9 302.2 %all-reduce.9.cloned.1.call-start = ((), (), s32[]{:S(2)}) async-start(), calls=%async_computation.2 | async-start | bytes 2097152 | tf_op jit(solution)/shard_map/psum | solution.py:14
  845.9 8.7 copy-start.2
  851.3 302.9 %all-reduce.11.cloned.1.call-start = ((), (), s32[]{:S(2)}) async-start(), calls=%async_computation.3 | async-start | bytes 2097152 | tf_op jit(solution)/shard_map/psum | solution.py:14
  854.6 148.6 %copy-start.7 = (bf16[512,1024]{1,0:T(8,128)(2,1)S(1)}, bf16[512,1024]{1,0:T(8,128)(2,1)}, u32[]{:S(2)}) copy-start(bf16[512,1024]{1,0:T(8,128)(2,1)} %all-gather.2.cloned.1.call-done) | copy-start | bytes 3145732
  1006.4 303.0 %all-reduce.13.cloned.1.call-start = ((), (), s32[]{:S(2)}) async-start(), calls=%async_computation.4 | async-start | bytes 2097152 | tf_op jit(solution)/shard_map/psum | solution.py:14
  1309.4 9.3 copy-start.1
Sparse Core Ops, SparseCore 0:
  505.2 21.5 all-gather.1
  697.0 148.8 all-reduce.6
  851.4 147.6 all-reduce.8
  1006.6 147.6 all-reduce.10
  1161.8 147.6 all-reduce.12
